TPU v7x, 32 devices: a whole 2x2x4 slice. The times are simulated.
32 devices in a mesh: seg: 2 (over x), ch: 16 (over z, y, core).
Axes of the slice: x: 2, y: 2, z: 4, core: 2. Of those that a mesh axis runs over, the one named last changes fastest.
Arguments:
- recording: bfloat16 [1024, 4096], P('ch', 'seg'), parts along dimension 1, may hold values from -300 to 300
- live_mask: int32 [4096], P('seg'), parts along dimension 0, may hold values 0 or 1
- window_starts: int32 [64], P('seg'), parts along dimension 0, may hold values from 0 to 512, as said below
- source_order: int32 [4], P('seg'), parts along dimension 0, may hold values from 0 to 15
Outputs:
- correlations: bfloat16 [2, 128, 4096, 128], P(None, None, ('seg', 'ch')), parts along dimension 2
There are 2 independent parts, one for each index of `seg`. A program takes and returns all parts, laid end to end along the dimension named above; each array names one. Nothing has to cross between parts.
Inputs may be any that keep to these rules, and one draw needn't show every extreme that they name: `window_starts`: the first start is 0 and the last is 512; the others are in no order and may repeat. `source_order`: block b is the channels b * 128 to (b + 1) * 128 - 1; blocks may repeat.
All inputs are finite; a program needn't handle non-finite values.
Results may differ from a plain program's by a relative error of at most 0.0059.
Values may be sent and summed in bfloat16 or wider, within the bound.
No kernel may reach another device: no remote copies, remote signals or barrier semaphores. Data moves between devices by JAX's collectives and lax.ppermute only.
A program may use at most 128 MiB of HBM per device.

v0:
```python
import math
import jax
import jax.numpy as jnp
from jax import lax
from jax.sharding import PartitionSpec as P

CH_DEV = 128
WIN = 512
NF = 128
F0 = 4
LAGS = 128
HALF = 64
BAND = 64
K = 2
NWIN = 32
STABILIZER_FLOOR = 1e-06


def broadcast(value, axis, source):
    kept = jnp.where(lax.axis_index(axis) == source, value, 0).astype(value.dtype)
    return lax.psum(kept, axis)


def banded(length, radius, number_type):
    row_index = jnp.arange(length)[:, None]
    col_index = jnp.arange(length)[None, :]
    return (jnp.abs(row_index - col_index) <= radius).astype(number_type)


def forward_table():
    phases = jnp.arange(WIN)[:, None] * (F0 + jnp.arange(NF))[None, :] % WIN
    angles = phases.astype(jnp.float32) * (2.0 * math.pi / WIN)
    return jnp.stack([jnp.cos(angles), -jnp.sin(angles)], axis=1).astype(jnp.bfloat16)


def inverse_table():
    phases = (F0 + jnp.arange(NF))[:, None] * (jnp.arange(LAGS)[None, :] - LAGS // 2) % WIN
    angles = phases.astype(jnp.float32) * (2.0 * math.pi / WIN)
    return jnp.stack([jnp.cos(angles), -jnp.sin(angles)], axis=0).astype(jnp.bfloat16)


def whiten(columns, window_starts, mask_portion):
    windows = jax.vmap(lambda start_shift: lax.dynamic_slice_in_dim(columns, start_shift, WIN, 0))(
        window_starts
    )
    values = windows.astype(jnp.float32)
    centred = values - jnp.mean(values, axis=1, keepdims=True)
    magnitude = jnp.abs(centred).astype(jnp.bfloat16)
    time_band = banded(WIN, HALF, jnp.bfloat16)
    time_counts = jnp.sum(time_band.astype(jnp.float32), axis=1)
    running = (
        jnp.einsum("jk,wkc->wjc", time_band, magnitude, preferred_element_type=jnp.float32)
        / time_counts[None, :, None]
    )
    normalized = (centred / (running + STABILIZER_FLOOR)).astype(jnp.bfloat16)
    channel_spectra = jnp.einsum(
        "wjc,jrf->wrfc", normalized, forward_table(), preferred_element_type=jnp.float32
    )
    amplitude = jnp.sqrt(
        channel_spectra[:, 0] * channel_spectra[:, 0]
        + channel_spectra[:, 1] * channel_spectra[:, 1]
    )
    bin_band = banded(NF, BAND, jnp.float32)
    smoothed_spectrum = (
        jnp.einsum("fg,wgc->wfc", bin_band, amplitude, precision=lax.Precision.HIGHEST)
        / jnp.sum(bin_band, axis=1)[None, :, None]
    )
    channel_alive_flags = mask_portion.astype(jnp.float32)
    return (
        channel_spectra / (smoothed_spectrum[:, None] + STABILIZER_FLOOR) * channel_alive_flags
    ).astype(jnp.bfloat16)


def stack_block(source, receivers, inverse):
    product = jnp.einsum("wrfs,wrfc->fsc", source, receivers, preferred_element_type=jnp.float32)
    cross_spec = (product / NWIN).astype(jnp.bfloat16)
    matched_pairs = cross_spec.reshape(NF, cross_spec.shape[1], 2, cross_spec.shape[2] // 2)
    lagged = jnp.einsum("fsrc,rft->sct", matched_pairs, inverse, preferred_element_type=jnp.float32)
    return (lagged * math.sqrt(NWIN / NF)).astype(jnp.bfloat16)


def local(recording, live_mask, window_starts, source_order):
    block_width = CH_DEV
    regrouped = lax.all_to_all(recording, "ch", split_axis=1, concat_axis=0, tiled=True)
    own_mask = lax.dynamic_slice_in_dim(
        live_mask, lax.axis_index("ch") * block_width, block_width, 0
    )
    whitened = whiten(regrouped, window_starts, own_mask)
    swapped = jnp.stack([whitened[:, 1], -whitened[:, 0]], axis=1)
    receivers = jnp.concatenate([whitened, swapped], axis=3)
    inverse = inverse_table()
    results = []
    for number in range(K):
        source = broadcast(whitened, "ch", source_order[number])
        results.append(stack_block(source, receivers, inverse))
    return jnp.stack(results)


def solution(mesh):
    in_specs = (P("ch", "seg"), P("seg"), P("seg"), P("seg"))
    out_specs = P(None, None, ("seg", "ch"), None)
    return jax.shard_map(local, mesh=mesh, in_specs=in_specs, out_specs=out_specs, check_vma=False)
```

profile of v0, /device:TPU:0, one launch (start us, length us, event | category | flops | bytes accessed | tf_op | source)
XLA Modules:
  0.0 295.2 jit_solution(15699077252839965585)
XLA Ops:
  8.3 7.4 %all-to-all-start = ((bf16[64,16,128]{2,0,1:T(8,128)(2,1)}), bf16[64,16,128]{2,0,1:T(8,128)(2,1)S(1)}, u32[]{:S(2)}, u32[]{:S(2)}) async-start(bf16[64,16,128]{2,0,1:T(8,128)(2,1)} %copy_bitcast_fusion), calls=%async_computation | async-start | bytes 524288 | tf_op jit(solution)/shard_map/all_to_all | solution.py:84
  21.2 4.5 %all-to-all-done = bf16[64,16,128]{2,0,1:T(8,128)(2,1)S(1)} async-done(((bf16[64,16,128]{2,0,1:T(8,128)(2,1)}), bf16[64,16,128]{2,0,1:T(8,128)(2,1)S(1)}, u32[]{:S(2)}, u32[]{:S(2)}) %all-to-all-start) | async-done | bytes 262176 | tf_op jit(solution)/shard_map/all_to_all | solution.py:84
  25.7 65.7 %while.1 = (s32[]{:T(128)}, bf16[1024,128]{1,0:T(8,128)(2,1)S(1)}, s32[32,2]{0,1:T(2,128)S(1)}, bf16[32,512,128]{2,1,0:T(8,128)(2,1)}, s32[]{:T(128)}) while((s32[]{:T(128)}, bf16[1024,128]{1,0:T(8,128)(2,1)S(1)}, s32[32,2]{0,1:T(2,128)S(1)}, bf16[32,512,128]{2,1,0:T(8,128)(2,1)}, s32[]{:T(128)}) %tuple.28), condition=%wide.while_cond, body=%wide.while_body.sunk | while | flops 2 | bytes 263257 | solution.py:43
  30.5 1.4 bitcast_dynamic-update-slice_fusion.2
  32.5 1.4 bitcast_dynamic-update-slice_fusion.2
  34.6 1.4 bitcast_dynamic-update-slice_fusion.2
  36.6 1.4 bitcast_dynamic-update-slice_fusion.2
  91.4 2.8 convert_reduce_fusion
  94.3 10.4 %fusion.16 = f32[32,2,128,128]{2,3,0,1:T(8,128)} fusion(f32[512]{0:T(512)S(1)} %convert_reduce_fusion.1, f32[32,128]{1,0:T(8,128)S(1)} %broadcast_multiply_fusion, bf16[32,512,128]{2,1,0:T(8,128)(2,1)} %get-tuple-element.12, bf16[512,1,128]{2,0,1:T(8,128)(2,1)S(1)} %get-tuple-element.32, bf16[512,1,128]{2,0,1:T(8,128)(2,1)S(1)} %get-tuple-element.31), kind=kOutput, calls=%fused_computation.25 | convolution fusion | flops 3243507712 | bytes 8669184 | tf_op jit(solution)/shard_map/wjc,jrf->wrfc/dot_general | solution.py:56
  104.6 4.1 %add_bitcast_fusion = f32[32,128,128]{1,2,0:T(8,128)S(1)} fusion(f32[32,2,128,128]{2,3,0,1:T(8,128)} %fusion.16, f32[128]{0:T(128)S(1)} %convert_reduce_fusion.2), kind=kOutput, calls=%fused_computation.32 | convolution fusion | flops 807976960 | bytes 6291968 | tf_op jit(solution)/shard_map/fg,wgc->wfc/dot_general | solution.py:65
  108.7 2.6 broadcast_select_fusion.1
  111.4 1.5 broadcast_select_fusion
  113.4 2.4 maximum_maximum_fusion
  115.8 8.1 %copy.16 = bf16[32,2,128,256]{3,0,1,2:T(8,128)(2,1)} copy(bf16[32,2,128,256]{2,3,0,1:T(8,128)(2,1)} %maximum_maximum_fusion) | data formatting | bytes 8388608 | tf_op jit(solution)/shard_map/concatenate | solution.py:90
  123.9 98.4 %all-reduce.4.cloned.1.call-done = (bf16[32,2,128,128]{2,3,0,1:T(8,128)(2,1)}, bf16[32,2,128,128]{2,3,0,1:T(8,128)(2,1)}) async-done(((bf16[32,2,128,128]{2,3,0,1:T(8,128)(2,1)}, bf16[32,2,128,128]{2,3,0,1:T(8,128)(2,1)}), (bf16[32,2,128,128]{2,3,0,1:T(8,128)(2,1)}, bf16[32,2,128,128]{2,3,0,1:T(8,128)(2,1)})) %all-reduce.4.cloned.1.call-update) | async-done | bytes 4194320 | tf_op jit(solution)/shard_map/psum | solution.py:21
  222.4 3.7 %copy.15 = bf16[32,2,128,128]{3,0,1,2:T(8,128)(2,1)S(1)} copy(bf16[32,2,128,128]{2,3,0,1:T(8,128)(2,1)} %get-tuple-element.22) | data formatting | bytes 4194304 | tf_op jit(solution)/shard_map/psum | solution.py:21
  226.0 8.0 %fusion.1 = bf16[128,128,256]{2,1,0:T(8,128)(2,1)} fusion(bf16[32,2,128,128]{3,0,1,2:T(8,128)(2,1)S(1)} %copy.15, bf16[32,2,128,256]{3,0,1,2:T(8,128)(2,1)} %copy.16), kind=kOutput, calls=%fused_computation.5 | convolution fusion | flops 545259520 | bytes 14680064 | tf_op jit(solution)/shard_map/wrfs,wrfc->fsc/dot_general | solution.py:75
  234.0 13.1 %copy.28 = bf16[128,128,256]{0,2,1:T(8,128)(2,1)} copy(bf16[128,128,256]{2,1,0:T(8,128)(2,1)} %fusion.1) | data formatting | bytes 16777216 | tf_op jit(solution)/shard_map/reshape | solution.py:77
  247.1 3.5 %copy.18 = bf16[32,2,128,128]{3,0,1,2:T(8,128)(2,1)S(1)} copy(bf16[32,2,128,128]{2,3,0,1:T(8,128)(2,1)} %get-tuple-element.21) | data formatting | bytes 4194304 | tf_op jit(solution)/shard_map/psum | solution.py:21
  250.6 8.0 %fusion = bf16[128,128,256]{2,1,0:T(8,128)(2,1)} fusion(bf16[32,2,128,128]{3,0,1,2:T(8,128)(2,1)S(1)} %copy.18, bf16[32,2,128,256]{3,0,1,2:T(8,128)(2,1)} %copy.16), kind=kOutput, calls=%fused_computation.3 | convolution fusion | flops 545259520 | bytes 14680064 | tf_op jit(solution)/shard_map/wrfs,wrfc->fsc/dot_general | solution.py:75
  258.6 13.1 %copy.29 = bf16[128,128,256]{0,2,1:T(8,128)(2,1)} copy(bf16[128,128,256]{2,1,0:T(8,128)(2,1)} %fusion) | data formatting | bytes 16777216 | tf_op jit(solution)/shard_map/reshape | solution.py:77
  271.7 5.9 %fusion.8 = bf16[1,128,128,128]{3,2,1,0:T(8,128)(2,1)S(1)} fusion(bf16[128,128,2,128]{0,3,2,1:T(8,128)(2,1)} %bitcast.92, bf16[1,128,128]{2,1,0:T(8,128)(2,1)S(1)} %get-tuple-element.28, bf16[1,128,128]{2,1,0:T(8,128)(2,1)S(1)} %get-tuple-element.27), kind=kOutput, calls=%fused_computation.17 | convolution fusion | flops 1077968896 | bytes 12648448 | tf_op jit(solution)/shard_map/fsrc,rft->sct/dot_general | solution.py:78
  277.6 4.3 %fusion.9 = bf16[1,128,128,128]{3,2,1,0:T(8,128)(2,1)} fusion(bf16[128,128,2,128]{0,3,2,1:T(8,128)(2,1)S(1)} %bitcast.93, bf16[1,128,128]{2,1,0:T(8,128)(2,1)S(1)} %get-tuple-element.28, bf16[1,128,128]{2,1,0:T(8,128)(2,1)S(1)} %get-tuple-element.27), kind=kOutput, calls=%fused_computation.18 | convolution fusion | flops 1077968896 | bytes 12648448 | tf_op jit(solution)/shard_map/fsrc,rft->sct/dot_general | solution.py:78
  281.9 6.4 %pad_maximum_fusion = bf16[2,128,128,128]{3,2,1,0:T(8,128)(2,1)} fusion(bf16[1,128,128,128]{3,2,1,0:T(8,128)(2,1)} %fusion.9, bf16[1,128,128,128]{3,2,1,0:T(8,128)(2,1)S(1)} %fusion.8), kind=kLoop, calls=%fused_computation.12 | loop fusion | flops 4194304 | bytes 16777216 | tf_op jit(solution)/shard_map/stack | solution.py:96
  (115 shorter events, 66.7 us)
Async XLA Ops:
  6.5 1.0 copy-start
  8.3 17.4 %all-to-all-start = ((bf16[64,16,128]{2,0,1:T(8,128)(2,1)}), bf16[64,16,128]{2,0,1:T(8,128)(2,1)S(1)}, u32[]{:S(2)}, u32[]{:S(2)}) async-start(bf16[64,16,128]{2,0,1:T(8,128)(2,1)} %copy_bitcast_fusion), calls=%async_computation | async-start | bytes 524288 | tf_op jit(solution)/shard_map/all_to_all | solution.py:84
  15.7 206.7 %all-reduce.4.cloned.1.call-start = ((), (), s32[]{:S(2)}) async-start(), calls=%async_computation.1 | async-start | bytes 8388608 | tf_op jit(solution)/shard_map/psum | solution.py:21
  104.6 4.1 %copy-start.3 = (f32[32,2,128,128]{2,3,0,1:T(8,128)S(1)}, f32[32,2,128,128]{2,3,0,1:T(8,128)}, u32[]{:S(2)}) copy-start(f32[32,2,128,128]{2,3,0,1:T(8,128)} %fusion.16) | copy-start | bytes 12582916
  271.7 5.9 %copy-start.2 = (bf16[128,128,256]{0,2,1:T(8,128)(2,1)S(1)}, bf16[128,128,256]{0,2,1:T(8,128)(2,1)}, u32[]{:S(2)}) copy-start(bf16[128,128,256]{0,2,1:T(8,128)(2,1)} %copy.29) | copy-start | bytes 25165828
  281.9 6.4 %copy-start.1 = (bf16[64,2048]{1,0:T(8,128)(2,1)S(1)}, bf16[64,2048]{1,0:T(8,128)(2,1)}, u32[]{:S(2)}) copy-start(bf16[64,2048]{1,0:T(8,128)(2,1)} %param.4) | copy-start | bytes 786436
Sparse Core Ops, SparseCore 0:
  113.0 109.3 all-reduce.3
where the time goes:
time: 297 us; the launch traced here: 295 us
  local copies, waits for them, and re-layouts  110 us (37%)
  waiting for transfers between devices  103 us (35%)
  matrix products  40.6 us (14%)
  other arithmetic  19.1 us (6%)
  between operations  14.8 us (5%)
  starting transfers between devices  7.45 us (3%)
    psum x1, waiting for transfers between devices, broadcast(): return lax.psum(kept, axis)  98.4 us
    gather x96, local copies, waits for them, and re-layouts  65.7 us
    reshape x2, local copies, waits for them, and re-layouts, stack_block(): cross_spec.reshape(NF, cross_spec.shape[1], 2, cross_spec.shape[2] // 2)  26.2 us
    dot_general x2, matrix products, stack_block(): jnp.einsum('wrfs,wrfc->fsc', source, receivers, preferred_element_type=jn...  15.9 us
    dot_general x1, matrix products, whiten(): jnp.einsum('wjc,jrf->wrfc', normalized, forward_table(), preferred_elemen...  10.4 us
    dot_general x2, matrix products, stack_block(): jnp.einsum('fsrc,rft->sct', matched_pairs, inverse, preferred_element_typ...  10.2 us
    concatenate x1, local copies, waits for them, and re-layouts, local(): receivers = jnp.concatenate([whitened, swapped], axis=3)  8.11 us
    all_to_all x1, starting transfers between devices, local(): lax.all_to_all(recording, 'ch', split_axis=1, concat_axis=0, tiled=True)  7.41 us
  transfers between devices with their start and end apart: 2, of which 2 were waited for; matrix products, arithmetic and copies ran while one was open for 5% of the time, Pallas kernels for 0%

commit v1 on v0

--- a/solution.py
+++ b/solution.py
@@ -3,6 +3,7 @@
 import jax.numpy as jnp
 from jax import lax
 from jax.sharding import PartitionSpec as P
+from jax.lax import all_gather
 
 CH_DEV = 128
 WIN = 512
@@ -18,7 +19,7 @@
 
 def broadcast(value, axis, source):
     kept = jnp.where(lax.axis_index(axis) == source, value, 0).astype(value.dtype)
-    return lax.psum(kept, axis)
+    return jnp.sum(all_gather(kept, axis), axis=0)
 
 
 def banded(length, radius, number_type):

time: 297 us -> 530 us (1.78)
  waiting for transfers between devices: 103 us -> 310 us
  other arithmetic: 19.1 us -> 46.6 us
    all_gather x0 -> x2, waiting for transfers between devices: none -> 305 us  [broadcast(): return jnp.sum(all_gather(kept, axis), axis=0)]
    psum x1 -> x0, waiting for transfers between devices: 98.4 us -> none  [broadcast(): return lax.psum(kept, axis)]
    reduce_sum x0 -> x2, other arithmetic: none -> 27.4 us  [broadcast(): return jnp.sum(all_gather(kept, axis), axis=0)]
    reduce_sum x0 -> x2, local copies, waits for them, and re-layouts: none -> 8.09 us  [broadcast(): return jnp.sum(all_gather(kept, axis), axis=0)]
    psum x2 -> x0, local copies, waits for them, and re-layouts: 7.17 us -> none  [broadcast(): return lax.psum(kept, axis)]
    gather x96 -> x160, local copies, waits for them, and re-layouts: 65.7 us -> 65.2 us
  transfers between devices with their start and end apart: 2 -> 3, of which waited for: 2 -> 3; matrix products, arithmetic and copies ran while one was open for 5% -> 7% of each run, Pallas kernels for 0% -> 0%
where the time goes in v1:
time: 530 us; the launch traced here: 529 us
  waiting for transfers between devices  310 us (58%)
  local copies, waits for them, and re-layouts  110 us (21%)
  other arithmetic  46.6 us (9%)
  matrix products  39 us (7%)
  between operations  14.8 us (3%)
  starting transfers between devices  7.68 us (1%)
    all_gather x2, waiting for transfers between devices, broadcast(): return jnp.sum(all_gather(kept, axis), axis=0)  305 us
    gather x160, local copies, waits for them, and re-layouts  65.2 us
    reduce_sum x2, other arithmetic, broadcast(): return jnp.sum(all_gather(kept, axis), axis=0)  27.4 us
    reshape x2, local copies, waits for them, and re-layouts, stack_block(): cross_spec.reshape(NF, cross_spec.shape[1], 2, cross_spec.shape[2] // 2)  25.8 us
    dot_general x2, matrix products, stack_block(): jnp.einsum('wrfs,wrfc->fsc', source, receivers, preferred_element_type=jn...  16.6 us
  transfers between devices with their start and end apart: 3, of which 3 were waited for; matrix products, arithmetic and copies ran while one was open for 7% of the time, Pallas kernels for 0%

profile of v1, /device:TPU:0, one launch (start us, length us, event | category | flops | bytes accessed | tf_op | source)
XLA Modules:
  0.0 528.6 jit_solution(5105508844299441457)
XLA Ops:
  8.2 7.4 %all-to-all-start = ((bf16[64,16,128]{2,0,1:T(8,128)(2,1)}), bf16[64,16,128]{2,0,1:T(8,128)(2,1)S(1)}, u32[]{:S(2)}, u32[]{:S(2)}) async-start(bf16[64,16,128]{2,0,1:T(8,128)(2,1)} %copy_bitcast_fusion), calls=%async_computation | async-start | bytes 524288 | tf_op jit(solution)/shard_map/all_to_all | solution.py:85
  16.4 1.3 fusion.57
  20.5 5.1 all-to-all-done
  25.7 65.7 %while.1 = (s32[]{:T(128)}, bf16[1024,128]{1,0:T(8,128)(2,1)S(1)}, s32[32,2]{0,1:T(2,128)S(1)}, bf16[32,512,128]{1,2,0:T(8,128)(2,1)}, s32[]{:T(128)}) while((s32[]{:T(128)}, bf16[1024,128]{1,0:T(8,128)(2,1)S(1)}, s32[32,2]{0,1:T(2,128)S(1)}, bf16[32,512,128]{1,2,0:T(8,128)(2,1)}, s32[]{:T(128)}) %tuple.29), condition=%wide.while_cond, body=%wide.while_body.sunk | while | flops 2 | bytes 786537 | solution.py:44
  91.4 2.8 convert_reduce_fusion
  94.2 8.2 %fusion.16 = f32[32,2,128,128]{2,3,0,1:T(8,128)} fusion(f32[512]{0:T(512)S(1)} %convert_reduce_fusion.1, f32[32,128]{1,0:T(8,128)S(1)} %broadcast_multiply_fusion, bf16[32,512,128]{1,2,0:T(8,128)(2,1)} %get-tuple-element.12, bf16[512,1,128]{2,0,1:T(8,128)(2,1)S(1)} %get-tuple-element.30, bf16[512,1,128]{2,0,1:T(8,128)(2,1)S(1)} %get-tuple-element.29), kind=kOutput, calls=%fused_computation.26 | convolution fusion | flops 3243507712 | bytes 8669184 | tf_op jit(solution)/shard_map/wjc,jrf->wrfc/dot_general | solution.py:57
  102.4 4.1 add_bitcast_fusion
  106.5 2.7 broadcast_select_fusion.1
  110.1 1.5 broadcast_select_fusion
  112.1 2.5 maximum_maximum_fusion
  114.6 8.1 %copy.22 = bf16[32,2,128,256]{3,0,1,2:T(8,128)(2,1)} copy(bf16[32,2,128,256]{2,3,0,1:T(8,128)(2,1)} %maximum_maximum_fusion) | data formatting | bytes 8388608 | tf_op jit(solution)/shard_map/concatenate | solution.py:91
  122.7 152.9 %all-gather.5.cloned.1.call-done = bf16[512,2,128,128]{2,3,0,1:T(8,128)(2,1)} async-done(((bf16[32,2,128,128]{2,3,0,1:T(8,128)(2,1)}), bf16[512,2,128,128]{2,3,0,1:T(8,128)(2,1)}) %all-gather.5.cloned.1.call-update) | async-done | bytes 33554448 | tf_op jit(solution)/shard_map/all_gather | solution.py:22
  275.6 14.4 %reduce_sum.54 = bf16[32,2,128,128]{2,3,0,1:T(8,128)(2,1)} reduce(bf16[16,32,2,128,128]{3,4,1,0,2:T(8,128)(2,1)} %bitcast.94, bf16[]{:T(256)} %constant.61.clone.1), dimensions={0}, to_apply=%region_3.4 | reduce | flops 15728640 | bytes 35651584 | tf_op jit(solution)/shard_map/reduce_sum | solution.py:22
  289.9 3.5 copy.21
  293.4 151.7 %all-gather.7.cloned.1.call-done = bf16[512,2,128,128]{2,3,0,1:T(8,128)(2,1)} async-done(((bf16[32,2,128,128]{2,3,0,1:T(8,128)(2,1)}), bf16[512,2,128,128]{2,3,0,1:T(8,128)(2,1)}) %all-gather.7.cloned.1.call-update) | async-done | bytes 33554448 | tf_op jit(solution)/shard_map/all_gather | solution.py:22
  445.2 13.1 %reduce_sum.55 = bf16[32,2,128,128]{2,3,0,1:T(8,128)(2,1)} reduce(bf16[16,32,2,128,128]{3,4,1,0,2:T(8,128)(2,1)} %bitcast.95, bf16[]{:T(256)} %constant.61.clone.1), dimensions={0}, to_apply=%region_4.5 | reduce | flops 15728640 | bytes 35651584 | tf_op jit(solution)/shard_map/reduce_sum | solution.py:22
  458.2 4.6 copy.24
  462.8 8.6 %fusion = bf16[128,128,256]{2,1,0:T(8,128)(2,1)} fusion(bf16[32,2,128,128]{3,0,1,2:T(8,128)(2,1)} %copy.24, bf16[32,2,128,256]{3,0,1,2:T(8,128)(2,1)} %copy.22), kind=kOutput, calls=%fused_computation.4 | convolution fusion | flops 545259520 | bytes 14680064 | tf_op jit(solution)/shard_map/wrfs,wrfc->fsc/dot_general | solution.py:76
  471.4 13.1 %copy.33 = bf16[128,128,256]{0,2,1:T(8,128)(2,1)} copy(bf16[128,128,256]{2,1,0:T(8,128)(2,1)} %fusion) | data formatting | bytes 16777216 | tf_op jit(solution)/shard_map/reshape | solution.py:78
  484.5 8.0 %fusion.1 = bf16[128,128,256]{2,1,0:T(8,128)(2,1)} fusion(bf16[32,2,128,128]{3,0,1,2:T(8,128)(2,1)S(1)} %copy.21, bf16[32,2,128,256]{3,0,1,2:T(8,128)(2,1)} %copy.22), kind=kOutput, calls=%fused_computation.6 | convolution fusion | flops 545259520 | bytes 14680064 | tf_op jit(solution)/shard_map/wrfs,wrfc->fsc/dot_general | solution.py:76
  492.5 12.7 %copy.32 = bf16[128,128,256]{0,2,1:T(8,128)(2,1)} copy(bf16[128,128,256]{2,1,0:T(8,128)(2,1)} %fusion.1) | data formatting | bytes 16777216 | tf_op jit(solution)/shard_map/reshape | solution.py:78
  505.2 5.9 %fusion.9 = bf16[1,128,128,128]{3,2,1,0:T(8,128)(2,1)S(1)} fusion(bf16[128,128,2,128]{0,3,2,1:T(8,128)(2,1)} %bitcast.96, bf16[1,128,128]{2,1,0:T(8,128)(2,1)S(1)} %get-tuple-element.26, bf16[1,128,128]{2,1,0:T(8,128)(2,1)S(1)} %get-tuple-element.25), kind=kOutput, calls=%fused_computation.19 | convolution fusion | flops 1077968896 | bytes 12648448 | tf_op jit(solution)/shard_map/fsrc,rft->sct/dot_general | solution.py:79
  511.1 4.3 fusion.8
  515.4 6.4 %pad_maximum_fusion = bf16[2,128,128,128]{3,2,1,0:T(8,128)(2,1)} fusion(bf16[1,128,128,128]{3,2,1,0:T(8,128)(2,1)S(1)} %fusion.9, bf16[1,128,128,128]{3,2,1,0:T(8,128)(2,1)} %fusion.8), kind=kLoop, calls=%fused_computation.13 | loop fusion | flops 4194304 | bytes 16777216 | tf_op jit(solution)/shard_map/stack | solution.py:97
  (184 shorter events, 70.6 us)
Async XLA Ops:
  6.5 1.0 copy-start
  8.2 17.4 %all-to-all-start = ((bf16[64,16,128]{2,0,1:T(8,128)(2,1)}), bf16[64,16,128]{2,0,1:T(8,128)(2,1)S(1)}, u32[]{:S(2)}, u32[]{:S(2)}) async-start(bf16[64,16,128]{2,0,1:T(8,128)(2,1)} %copy_bitcast_fusion), calls=%async_computation | async-start | bytes 524288 | tf_op jit(solution)/shard_map/all_to_all | solution.py:85
  15.7 259.9 %all-gather.5.cloned.1.call-start = ((), (), s32[]{:S(2)}) async-start(), calls=%async_computation.1 | async-start | bytes 35651584 | tf_op jit(solution)/shard_map/all_gather | solution.py:22
  102.4 4.1 copy-start.3
  109.2 336.0 %all-gather.7.cloned.1.call-start = ((), (), s32[]{:S(2)}) async-start(), calls=%async_computation.2 | async-start | bytes 35651584 | tf_op jit(solution)/shard_map/all_gather | solution.py:22
  505.2 5.9 %copy-start.2 = (bf16[128,128,256]{0,2,1:T(8,128)(2,1)S(1)}, bf16[128,128,256]{0,2,1:T(8,128)(2,1)}, u32[]{:S(2)}) copy-start(bf16[128,128,256]{0,2,1:T(8,128)(2,1)} %copy.32) | copy-start | bytes 25165828
  515.4 6.4 %copy-start.1 = (bf16[64,2048]{1,0:T(8,128)(2,1)S(1)}, bf16[64,2048]{1,0:T(8,128)(2,1)}, u32[]{:S(2)}) copy-start(bf16[64,2048]{1,0:T(8,128)(2,1)} %param.4) | copy-start | bytes 786436
Sparse Core Ops, SparseCore 0:
  109.3 166.2 all-gather.4
  277.1 168.0 all-gather.6
